TPU v7x, 32 devices: a whole 2x2x4 slice. The times are simulated.
32 devices in a mesh: dp: 8 (over z, core), feat: 4 (over y, x).
Axes of the slice: x: 2, y: 2, z: 4, core: 2. Of those that a mesh axis runs over, the one named last changes fastest.
Arguments:
- bins: int32 [512, 24576], P('feat', 'dp'), may hold values from 0 to 255, as said below
- grads: float32 [8, 24576], P(None, 'dp'), may hold values from -6 to 6
- hess: float32 [8, 24576], P(None, 'dp'), may hold values from 0.05 to 1
- nodes: int32 [24576], P('dp'), may hold values from 0 to 3
- row_count: int32 [8], P('dp'), may hold values from 1 to 3072, 15360 in all
Outputs:
- best_gain: float32 [4, 512], P(None, 'feat')
Inputs may be any that keep to these rules, and one draw needn't show every extreme that they name: Row slots at or beyond row_count of their dp index are padding; the counts of all dp indices add up to 5 / 8 of 24576. `bins`: each entry is a bin of its feature.
All inputs are finite; a program needn't handle non-finite values. No bound on the sum of `row_count` on one device may be relied on, other than what follows from the above.
Results may differ from a plain program's by a relative error of at most 0.0016.
Values sent between devices are 32-bit elements; how exact they have to be, the bound alone decides.
A program may use at most 64 MiB of HBM per device.

v0:
```python
import math

import jax
import jax.numpy as jnp
from jax import lax
from jax.sharding import PartitionSpec as P

BINS = 256
OUT = 8
NODES = 4


def split_score(sums):
    shaped = sums.reshape(sums.shape[:-1] + (NODES, 2, OUT))
    grad_sum = shaped[..., 0, :]
    hess_sum = shaped[..., 1, :]
    return jnp.sum(grad_sum * grad_sum / (hess_sum + 1.0), axis=-1)


def split_gain(left_sums, all_sums):
    return split_score(left_sums) + split_score(all_sums - left_sums) - split_score(all_sums)


def shards(bins, grads, hess, nodes, row_count):
    feat_dev, capacity = bins.shape
    col_width = NODES * 2 * OUT
    row_block = min(1024, capacity)
    live_count = row_count[0]
    node_labels = lax.broadcasted_iota(jnp.int32, (NODES, 1), 0)
    grad_pairs = jnp.concatenate([grads, hess], axis=0).astype(jnp.bfloat16)

    def block_weights(row_start):
        slot_index = row_start + lax.broadcasted_iota(jnp.int32, (1, row_block), 1)
        node_block = lax.dynamic_slice_in_dim(nodes, row_start, row_block, 0)
        member = (node_block[None, :] == node_labels) & (slot_index < live_count)
        pair_stats = lax.dynamic_slice_in_dim(grad_pairs, row_start, row_block, 1)
        weighted = jnp.where(
            member[:, None, :], pair_stats[None, :, :], jnp.zeros((), jnp.bfloat16)
        )
        return weighted.reshape(col_width, row_block)

    own_count = feat_dev // lax.axis_size("dp")
    feat_count = lax.axis_size("dp") * own_count
    feat_group = math.gcd(feat_count, 16)
    levels = lax.broadcasted_iota(jnp.int32, (1, BINS, 1), 1)

    def one_block(block_index, histogram):
        row_start = block_index * row_block
        weighted = block_weights(row_start)

        def one_group(group_index, hist_acc):
            feat_first = group_index * feat_group
            bin_codes = lax.dynamic_slice(bins, (feat_first, row_start), (feat_group, row_block))
            onehot = (bin_codes[:, None, :] == levels).astype(jnp.bfloat16)
            partial_sum = jnp.einsum(
                "cr,fbr->cfb", weighted, onehot, preferred_element_type=jnp.float32
            )
            corner = (0, feat_first, 0)
            current = lax.dynamic_slice(hist_acc, corner, partial_sum.shape)
            return lax.dynamic_update_slice(hist_acc, current + partial_sum, corner)

        return lax.fori_loop(0, feat_count // feat_group, one_group, histogram)

    n_blocks = capacity // row_block
    summed = lax.fori_loop(
        0, n_blocks, one_block, jnp.zeros((col_width, feat_count, BINS), jnp.float32)
    )
    histogram = lax.psum_scatter(
        summed.transpose(1, 2, 0).reshape(feat_count, BINS * col_width),
        "dp",
        scatter_dimension=0,
        tiled=True,
    )
    left_sums = jnp.cumsum(histogram.reshape(own_count, BINS, col_width), axis=1)
    split_gains = split_gain(left_sums, left_sums[:, -1:, :])
    own_best = jnp.max(split_gains, axis=1).T
    best_gain = lax.all_gather(own_best, "dp", axis=1, tiled=True)
    return best_gain


def solution(mesh):
    in_specs = (P("feat", "dp"), P(None, "dp"), P(None, "dp"), P("dp"), P("dp"))
    out_specs = P(None, "feat")
    return jax.shard_map(shards, mesh=mesh, in_specs=in_specs, out_specs=out_specs, check_vma=False)
```

profile of v0, /device:TPU:0, one launch (start us, length us, event | category | flops | bytes accessed | tf_op | source)
XLA Modules:
  0.0 322.1 jit_solution(14840188867906533278)
XLA Ops:
  12.6 151.6 %while.41 = (s32[]{:T(128)}, f32[64,128,256]{2,0,1:T(8,128)}, s32[3072]{0:T(1024)}, s32[]{:T(128)}, bf16[16,3072]{1,0:T(8,128)(2,1)S(1)}, /*index=5*/s32[128,307...) while((s32[]{:T(128)}, f32[64,128,256]{2,0,1:T(8,128)}, ...), condition=%wide.region_3.4_spmd.clone, body=%wide.region_0.3_spmd.clone.sunk | while | flops 541403136 | bytes 2679238 | solution.py:65
  14.0 49.1 %while.42 = (s32[]{:T(128)}, f32[64,128,256]{2,0,1:T(8,128)}, s32[128,3072]{1,0:T(8,128)}, s32[]{:T(128)}, s32[1,256,1]{1,2,0:T(1,128)S(1)}, /*index=5*/bf16[16,...) while((s32[]{:T(128)}, f32[64,128,256]{2,0,1:T(8,128)}, ...), condition=%wide.region_2.2_spmd.clone, body=%wide.region_1.1_spmd.clone.sunk | while | flops 541392896 | bytes 2593955 | solution.py:62
  14.9 5.3 %fusion.38 = f32[64,128,256]{2,0,1:T(8,128)} fusion(f32[64,128,256]{2,0,1:T(8,128)} %get-tuple-element.488, s32[]{:T(128)S(6)} %select_n.54, bf16[64,1024,1]{1,0,2:T(8,128)(2,1)S(1)} %bitcast.54, s32[16,1024]{1,0:T(8,128)S(1)} %dynamic_slice.43, s32[256]{0:T(256)S(1)} %bitcast.61), kind=kOutput, calls=%fused_computation.9.clone.1 | convolution fusion | flops 541327360 | bytes 2294788 | tf_op jit(solution)/shard_map/while/body/eval_jaxpr/while/body/eval_jaxpr/cr,fbr->cfb/dot_general | solution.py:55
  21.1 5.3 %fusion.38 = f32[64,128,256]{2,0,1:T(8,128)} fusion(f32[64,128,256]{2,0,1:T(8,128)} %get-tuple-element.488, s32[]{:T(128)S(6)} %select_n.54, bf16[64,1024,1]{1,0,2:T(8,128)(2,1)S(1)} %bitcast.54, s32[16,1024]{1,0:T(8,128)S(1)} %dynamic_slice.43, s32[256]{0:T(256)S(1)} %bitcast.61), kind=kOutput, calls=%fused_computation.9.clone.1 | convolution fusion | flops 541327360 | bytes 2294788 | tf_op jit(solution)/shard_map/while/body/eval_jaxpr/while/body/eval_jaxpr/cr,fbr->cfb/dot_general | solution.py:55
  27.2 5.3 %fusion.38 = f32[64,128,256]{2,0,1:T(8,128)} fusion(f32[64,128,256]{2,0,1:T(8,128)} %get-tuple-element.488, s32[]{:T(128)S(6)} %select_n.54, bf16[64,1024,1]{1,0,2:T(8,128)(2,1)S(1)} %bitcast.54, s32[16,1024]{1,0:T(8,128)S(1)} %dynamic_slice.43, s32[256]{0:T(256)S(1)} %bitcast.61), kind=kOutput, calls=%fused_computation.9.clone.1 | convolution fusion | flops 541327360 | bytes 2294788 | tf_op jit(solution)/shard_map/while/body/eval_jaxpr/while/body/eval_jaxpr/cr,fbr->cfb/dot_general | solution.py:55
  33.4 5.3 %fusion.38 = f32[64,128,256]{2,0,1:T(8,128)} fusion(f32[64,128,256]{2,0,1:T(8,128)} %get-tuple-element.488, s32[]{:T(128)S(6)} %select_n.54, bf16[64,1024,1]{1,0,2:T(8,128)(2,1)S(1)} %bitcast.54, s32[16,1024]{1,0:T(8,128)S(1)} %dynamic_slice.43, s32[256]{0:T(256)S(1)} %bitcast.61), kind=kOutput, calls=%fused_computation.9.clone.1 | convolution fusion | flops 541327360 | bytes 2294788 | tf_op jit(solution)/shard_map/while/body/eval_jaxpr/while/body/eval_jaxpr/cr,fbr->cfb/dot_general | solution.py:55
  45.6 5.3 %fusion.38 = f32[64,128,256]{2,0,1:T(8,128)} fusion(f32[64,128,256]{2,0,1:T(8,128)} %get-tuple-element.488, s32[]{:T(128)S(6)} %select_n.54, bf16[64,1024,1]{1,0,2:T(8,128)(2,1)S(1)} %bitcast.54, s32[16,1024]{1,0:T(8,128)S(1)} %dynamic_slice.43, s32[256]{0:T(256)S(1)} %bitcast.61), kind=kOutput, calls=%fused_computation.9.clone.1 | convolution fusion | flops 541327360 | bytes 2294788 | tf_op jit(solution)/shard_map/while/body/eval_jaxpr/while/body/eval_jaxpr/cr,fbr->cfb/dot_general | solution.py:55
  51.8 5.3 %fusion.38 = f32[64,128,256]{2,0,1:T(8,128)} fusion(f32[64,128,256]{2,0,1:T(8,128)} %get-tuple-element.488, s32[]{:T(128)S(6)} %select_n.54, bf16[64,1024,1]{1,0,2:T(8,128)(2,1)S(1)} %bitcast.54, s32[16,1024]{1,0:T(8,128)S(1)} %dynamic_slice.43, s32[256]{0:T(256)S(1)} %bitcast.61), kind=kOutput, calls=%fused_computation.9.clone.1 | convolution fusion | flops 541327360 | bytes 2294788 | tf_op jit(solution)/shard_map/while/body/eval_jaxpr/while/body/eval_jaxpr/cr,fbr->cfb/dot_general | solution.py:55
  57.9 5.2 %fusion.38 = f32[64,128,256]{2,0,1:T(8,128)} fusion(f32[64,128,256]{2,0,1:T(8,128)} %get-tuple-element.488, s32[]{:T(128)S(6)} %select_n.54, bf16[64,1024,1]{1,0,2:T(8,128)(2,1)S(1)} %bitcast.54, s32[16,1024]{1,0:T(8,128)S(1)} %dynamic_slice.43, s32[256]{0:T(256)S(1)} %bitcast.61), kind=kOutput, calls=%fused_computation.9.clone.1 | convolution fusion | flops 541327360 | bytes 2294788 | tf_op jit(solution)/shard_map/while/body/eval_jaxpr/while/body/eval_jaxpr/cr,fbr->cfb/dot_general | solution.py:55
  64.5 49.1 %while.42 = (s32[]{:T(128)}, f32[64,128,256]{2,0,1:T(8,128)}, s32[128,3072]{1,0:T(8,128)}, s32[]{:T(128)}, s32[1,256,1]{1,2,0:T(1,128)S(1)}, /*index=5*/bf16[16,...) while((s32[]{:T(128)}, f32[64,128,256]{2,0,1:T(8,128)}, ...), condition=%wide.region_2.2_spmd.clone, body=%wide.region_1.1_spmd.clone.sunk | while | flops 541392896 | bytes 2593955 | solution.py:62
  65.4 5.3 %fusion.38 = f32[64,128,256]{2,0,1:T(8,128)} fusion(f32[64,128,256]{2,0,1:T(8,128)} %get-tuple-element.488, s32[]{:T(128)S(6)} %select_n.54, bf16[64,1024,1]{1,0,2:T(8,128)(2,1)S(1)} %bitcast.54, s32[16,1024]{1,0:T(8,128)S(1)} %dynamic_slice.43, s32[256]{0:T(256)S(1)} %bitcast.61), kind=kOutput, calls=%fused_computation.9.clone.1 | convolution fusion | flops 541327360 | bytes 2294788 | tf_op jit(solution)/shard_map/while/body/eval_jaxpr/while/body/eval_jaxpr/cr,fbr->cfb/dot_general | solution.py:55
  71.6 5.3 %fusion.38 = f32[64,128,256]{2,0,1:T(8,128)} fusion(f32[64,128,256]{2,0,1:T(8,128)} %get-tuple-element.488, s32[]{:T(128)S(6)} %select_n.54, bf16[64,1024,1]{1,0,2:T(8,128)(2,1)S(1)} %bitcast.54, s32[16,1024]{1,0:T(8,128)S(1)} %dynamic_slice.43, s32[256]{0:T(256)S(1)} %bitcast.61), kind=kOutput, calls=%fused_computation.9.clone.1 | convolution fusion | flops 541327360 | bytes 2294788 | tf_op jit(solution)/shard_map/while/body/eval_jaxpr/while/body/eval_jaxpr/cr,fbr->cfb/dot_general | solution.py:55
  77.8 5.3 %fusion.38 = f32[64,128,256]{2,0,1:T(8,128)} fusion(f32[64,128,256]{2,0,1:T(8,128)} %get-tuple-element.488, s32[]{:T(128)S(6)} %select_n.54, bf16[64,1024,1]{1,0,2:T(8,128)(2,1)S(1)} %bitcast.54, s32[16,1024]{1,0:T(8,128)S(1)} %dynamic_slice.43, s32[256]{0:T(256)S(1)} %bitcast.61), kind=kOutput, calls=%fused_computation.9.clone.1 | convolution fusion | flops 541327360 | bytes 2294788 | tf_op jit(solution)/shard_map/while/body/eval_jaxpr/while/body/eval_jaxpr/cr,fbr->cfb/dot_general | solution.py:55
  83.9 5.3 %fusion.38 = f32[64,128,256]{2,0,1:T(8,128)} fusion(f32[64,128,256]{2,0,1:T(8,128)} %get-tuple-element.488, s32[]{:T(128)S(6)} %select_n.54, bf16[64,1024,1]{1,0,2:T(8,128)(2,1)S(1)} %bitcast.54, s32[16,1024]{1,0:T(8,128)S(1)} %dynamic_slice.43, s32[256]{0:T(256)S(1)} %bitcast.61), kind=kOutput, calls=%fused_computation.9.clone.1 | convolution fusion | flops 541327360 | bytes 2294788 | tf_op jit(solution)/shard_map/while/body/eval_jaxpr/while/body/eval_jaxpr/cr,fbr->cfb/dot_general | solution.py:55
  96.1 5.3 %fusion.38 = f32[64,128,256]{2,0,1:T(8,128)} fusion(f32[64,128,256]{2,0,1:T(8,128)} %get-tuple-element.488, s32[]{:T(128)S(6)} %select_n.54, bf16[64,1024,1]{1,0,2:T(8,128)(2,1)S(1)} %bitcast.54, s32[16,1024]{1,0:T(8,128)S(1)} %dynamic_slice.43, s32[256]{0:T(256)S(1)} %bitcast.61), kind=kOutput, calls=%fused_computation.9.clone.1 | convolution fusion | flops 541327360 | bytes 2294788 | tf_op jit(solution)/shard_map/while/body/eval_jaxpr/while/body/eval_jaxpr/cr,fbr->cfb/dot_general | solution.py:55
  102.3 5.3 %fusion.38 = f32[64,128,256]{2,0,1:T(8,128)} fusion(f32[64,128,256]{2,0,1:T(8,128)} %get-tuple-element.488, s32[]{:T(128)S(6)} %select_n.54, bf16[64,1024,1]{1,0,2:T(8,128)(2,1)S(1)} %bitcast.54, s32[16,1024]{1,0:T(8,128)S(1)} %dynamic_slice.43, s32[256]{0:T(256)S(1)} %bitcast.61), kind=kOutput, calls=%fused_computation.9.clone.1 | convolution fusion | flops 541327360 | bytes 2294788 | tf_op jit(solution)/shard_map/while/body/eval_jaxpr/while/body/eval_jaxpr/cr,fbr->cfb/dot_general | solution.py:55
  108.4 5.2 %fusion.38 = f32[64,128,256]{2,0,1:T(8,128)} fusion(f32[64,128,256]{2,0,1:T(8,128)} %get-tuple-element.488, s32[]{:T(128)S(6)} %select_n.54, bf16[64,1024,1]{1,0,2:T(8,128)(2,1)S(1)} %bitcast.54, s32[16,1024]{1,0:T(8,128)S(1)} %dynamic_slice.43, s32[256]{0:T(256)S(1)} %bitcast.61), kind=kOutput, calls=%fused_computation.9.clone.1 | convolution fusion | flops 541327360 | bytes 2294788 | tf_op jit(solution)/shard_map/while/body/eval_jaxpr/while/body/eval_jaxpr/cr,fbr->cfb/dot_general | solution.py:55
  115.1 49.1 %while.42 = (s32[]{:T(128)}, f32[64,128,256]{2,0,1:T(8,128)}, s32[128,3072]{1,0:T(8,128)}, s32[]{:T(128)}, s32[1,256,1]{1,2,0:T(1,128)S(1)}, /*index=5*/bf16[16,...) while((s32[]{:T(128)}, f32[64,128,256]{2,0,1:T(8,128)}, ...), condition=%wide.region_2.2_spmd.clone, body=%wide.region_1.1_spmd.clone.sunk | while | flops 541392896 | bytes 2593955 | solution.py:62
  116.0 5.3 %fusion.38 = f32[64,128,256]{2,0,1:T(8,128)} fusion(f32[64,128,256]{2,0,1:T(8,128)} %get-tuple-element.488, s32[]{:T(128)S(6)} %select_n.54, bf16[64,1024,1]{1,0,2:T(8,128)(2,1)S(1)} %bitcast.54, s32[16,1024]{1,0:T(8,128)S(1)} %dynamic_slice.43, s32[256]{0:T(256)S(1)} %bitcast.61), kind=kOutput, calls=%fused_computation.9.clone.1 | convolution fusion | flops 541327360 | bytes 2294788 | tf_op jit(solution)/shard_map/while/body/eval_jaxpr/while/body/eval_jaxpr/cr,fbr->cfb/dot_general | solution.py:55
  122.1 5.3 %fusion.38 = f32[64,128,256]{2,0,1:T(8,128)} fusion(f32[64,128,256]{2,0,1:T(8,128)} %get-tuple-element.488, s32[]{:T(128)S(6)} %select_n.54, bf16[64,1024,1]{1,0,2:T(8,128)(2,1)S(1)} %bitcast.54, s32[16,1024]{1,0:T(8,128)S(1)} %dynamic_slice.43, s32[256]{0:T(256)S(1)} %bitcast.61), kind=kOutput, calls=%fused_computation.9.clone.1 | convolution fusion | flops 541327360 | bytes 2294788 | tf_op jit(solution)/shard_map/while/body/eval_jaxpr/while/body/eval_jaxpr/cr,fbr->cfb/dot_general | solution.py:55
  128.3 5.3 %fusion.38 = f32[64,128,256]{2,0,1:T(8,128)} fusion(f32[64,128,256]{2,0,1:T(8,128)} %get-tuple-element.488, s32[]{:T(128)S(6)} %select_n.54, bf16[64,1024,1]{1,0,2:T(8,128)(2,1)S(1)} %bitcast.54, s32[16,1024]{1,0:T(8,128)S(1)} %dynamic_slice.43, s32[256]{0:T(256)S(1)} %bitcast.61), kind=kOutput, calls=%fused_computation.9.clone.1 | convolution fusion | flops 541327360 | bytes 2294788 | tf_op jit(solution)/shard_map/while/body/eval_jaxpr/while/body/eval_jaxpr/cr,fbr->cfb/dot_general | solution.py:55
  134.4 5.3 %fusion.38 = f32[64,128,256]{2,0,1:T(8,128)} fusion(f32[64,128,256]{2,0,1:T(8,128)} %get-tuple-element.488, s32[]{:T(128)S(6)} %select_n.54, bf16[64,1024,1]{1,0,2:T(8,128)(2,1)S(1)} %bitcast.54, s32[16,1024]{1,0:T(8,128)S(1)} %dynamic_slice.43, s32[256]{0:T(256)S(1)} %bitcast.61), kind=kOutput, calls=%fused_computation.9.clone.1 | convolution fusion | flops 541327360 | bytes 2294788 | tf_op jit(solution)/shard_map/while/body/eval_jaxpr/while/body/eval_jaxpr/cr,fbr->cfb/dot_general | solution.py:55
  146.6 5.3 %fusion.38 = f32[64,128,256]{2,0,1:T(8,128)} fusion(f32[64,128,256]{2,0,1:T(8,128)} %get-tuple-element.488, s32[]{:T(128)S(6)} %select_n.54, bf16[64,1024,1]{1,0,2:T(8,128)(2,1)S(1)} %bitcast.54, s32[16,1024]{1,0:T(8,128)S(1)} %dynamic_slice.43, s32[256]{0:T(256)S(1)} %bitcast.61), kind=kOutput, calls=%fused_computation.9.clone.1 | convolution fusion | flops 541327360 | bytes 2294788 | tf_op jit(solution)/shard_map/while/body/eval_jaxpr/while/body/eval_jaxpr/cr,fbr->cfb/dot_general | solution.py:55
  152.8 5.3 %fusion.38 = f32[64,128,256]{2,0,1:T(8,128)} fusion(f32[64,128,256]{2,0,1:T(8,128)} %get-tuple-element.488, s32[]{:T(128)S(6)} %select_n.54, bf16[64,1024,1]{1,0,2:T(8,128)(2,1)S(1)} %bitcast.54, s32[16,1024]{1,0:T(8,128)S(1)} %dynamic_slice.43, s32[256]{0:T(256)S(1)} %bitcast.61), kind=kOutput, calls=%fused_computation.9.clone.1 | convolution fusion | flops 541327360 | bytes 2294788 | tf_op jit(solution)/shard_map/while/body/eval_jaxpr/while/body/eval_jaxpr/cr,fbr->cfb/dot_general | solution.py:55
  159.0 5.2 %fusion.38 = f32[64,128,256]{2,0,1:T(8,128)} fusion(f32[64,128,256]{2,0,1:T(8,128)} %get-tuple-element.488, s32[]{:T(128)S(6)} %select_n.54, bf16[64,1024,1]{1,0,2:T(8,128)(2,1)S(1)} %bitcast.54, s32[16,1024]{1,0:T(8,128)S(1)} %dynamic_slice.43, s32[256]{0:T(256)S(1)} %bitcast.61), kind=kOutput, calls=%fused_computation.9.clone.1 | convolution fusion | flops 541327360 | bytes 2294788 | tf_op jit(solution)/shard_map/while/body/eval_jaxpr/while/body/eval_jaxpr/cr,fbr->cfb/dot_general | solution.py:55
  164.2 8.9 %copy.25 = f32[64,128,256]{1,0,2:T(8,128)} copy(f32[64,128,256]{2,0,1:T(8,128)} %get-tuple-element.304) | data formatting | bytes 16777216 | tf_op jit(solution)/shard_map/while | solution.py:65
  173.1 9.0 %copy.40 = f32[128,16384]{1,0:T(8,128)} copy(f32[128,16384]{0,1:T(8,128)} %bitcast.56) | data formatting | bytes 16777216
  182.1 92.5 %reduce-scatter.4.cloned.1.call-done = f32[16,16384]{1,0:T(8,128)} async-done(((f32[128,16384]{1,0:T(8,128)}), f32[16,16384]{1,0:T(8,128)}) %reduce-scatter.4.cloned.1.call-update) | async-done | bytes 1048592
  274.6 5.9 %copy.41 = f32[16,16384]{0,1:T(8,128)} copy(f32[16,16384]{1,0:T(8,128)} %reduce-scatter.4.cloned.1.call-done) | data formatting | bytes 2097152
  280.5 6.8 %copy.28 = f32[16,64,2,128]{3,1,2,0:T(8,128)S(1)} copy(f32[16,64,2,128]{0,1,3,2:T(8,128)} %bitcast.55) | data formatting | bytes 2097152 | tf_op jit(solution)/shard_map/reshape.3
  287.4 9.5 %reduce-window.6 = f32[16,64,2,128]{3,1,2,0:T(8,128)S(1)} reduce-window(f32[16,64,2,128]{3,1,2,0:T(8,128)S(1)} %copy.28, f32[]{:T(128)} %constant.85.clone.1), window={size=1x1x1x128 pad=0_0x0_0x0_0x127_0}, to_apply=%region_5.6 | reduce-window | flops 33292288 | bytes 2097156 | tf_op jit(solution)/shard_map/reduce-window
  301.9 12.7 %all-gather = f32[8,16,4]{1,2,0:T(4,128)S(1)} all-gather(f32[1,16,4]{1,2,0:T(4,128)S(1)} %bitcast.60), channel_id=1, replica_groups=mesh['dp'=8,'feat'=4] {'dp'}, dimensions={0}, use_global_device_ids=true | all-gather | bytes 2304 | tf_op jit(solution)/shard_map/all_gather | solution.py:77
  (88 shorter events, 52.4 us)
Async XLA Ops:
  6.5 268.1 %reduce-scatter.4.cloned.1.call-start = ((), (), s32[]{:S(2)}) async-start(), calls=%async_computation.1 | async-start | bytes 9437184
Sparse Core Ops, SparseCore 0:
  182.2 92.3 reduce-scatter.3
where the time goes:
time: 325 us; the launch traced here: 322 us
  matrix products  126 us (39%)
  waiting for transfers between devices  92.5 us (28%)
  local copies, waits for them, and re-layouts  61.4 us (19%)
  other arithmetic  15.4 us (5%)
  between operations  13.4 us (4%)
  blocking collectives  12.7 us (4%)
    dot_general x24, matrix products, one_group(): jnp.einsum('cr,fbr->cfb', weighted, onehot, preferred_element_type=jnp.fl...  126 us
    unnamed x2, waiting for transfers between devices  92.5 us
    dynamic_slice x24, local copies, waits for them, and re-layouts, one_group(): lax.dynamic_slice(bins, (feat_first, row_start), (feat_group, row_block))  20.3 us
    unnamed x3, local copies, waits for them, and re-layouts  15.6 us
    all_gather x1, blocking collectives, shards(): best_gain = lax.all_gather(own_best, 'dp', axis=1, tiled=True)  12.7 us
    another operation x5, other arithmetic  11.7 us
    while x1, local copies, waits for them, and re-layouts, shards(): lax.fori_loop(0, n_blocks, one_block, jnp.zeros((col_width, feat_count, B...  8.86 us
    another operation x3, local copies, waits for them, and re-layouts  6.86 us
  transfers between devices with their start and end apart: 1, of which 1 were waited for; matrix products, arithmetic and copies ran while one was open for 0% of the time, Pallas kernels for 0%

commit v1 on v0

v1 whole, which is shorter than its diff:
```python
import functools

import jax
import jax.numpy as jnp
from jax import lax
from jax.experimental import pallas as pl
from jax.experimental.pallas import tpu as pltpu
from jax.sharding import PartitionSpec as P

BINS = 256
OUT = 8
NODES = 4
PAIR = 2 * OUT
COLS = NODES * PAIR
HIGH = BINS // 2
LANES = 128
ROW_TILE = 512
OVER_LANES = (((1,), (1,)), ((), ()))


def score(sums):
    shaped = sums.reshape(NODES, PAIR, sums.shape[-1])
    grad_sum = shaped[:, :OUT, :]
    hess_sum = shaped[:, OUT:, :]
    return jnp.sum(grad_sum * grad_sum / (hess_sum + 1.0), axis=1)


def kernel(n, bins_ref, grads_ref, hess_ref, nodes_ref, count_ref, out_ref,
           bins_all, stats_all, nodes_all, weights, left_acc, gain_all,
           own_sem, bins_send, bins_recv, stats_send, stats_recv,
           nodes_send, nodes_recv, gain_send, gain_recv):
    own, rows = bins_all.shape[1:]
    me = lax.axis_index("dp")

    def partner(k):
        other, bit = 0, 1
        while bit < n:
            other = other + ((me // bit + k // bit) % 2) * bit
            bit *= 2
        return other

    def remote(src, dst, send, recv, k):
        return pltpu.make_async_remote_copy(
            src_ref=src, dst_ref=dst, send_sem=send.at[k], recv_sem=recv.at[k],
            device_id={"dp": partner(k)}, device_id_type=pl.DeviceIdType.MESH)

    def bins_copy(k):
        return remote(bins_ref.at[partner(k)], bins_all.at[k], bins_send, bins_recv, k)

    def stats_copy(k):
        return remote(stats_all.at[0], stats_all.at[k], stats_send, stats_recv, k)

    def nodes_copy(k):
        return remote(nodes_all.at[0], nodes_all.at[k], nodes_send, nodes_recv, k)

    def gain_copy(k):
        return remote(gain_all.at[0], gain_all.at[k], gain_send, gain_recv, k)

    own_copy = pltpu.make_async_copy(bins_ref.at[me], bins_all.at[0], own_sem)
    own_copy.start()
    barrier = pltpu.get_barrier_semaphore()

    @pl.loop(1, n)
    def _(k):
        pl.semaphore_signal(barrier, inc=1, device_id={"dp": partner(k)},
                            device_id_type=pl.DeviceIdType.MESH)

    slot_index = lax.broadcasted_iota(jnp.int32, (1, rows), 1)
    nodes_all[0] = jnp.where(slot_index < count_ref[0], nodes_ref[...], NODES)
    stats_all[0, :OUT] = grads_ref[...]
    stats_all[0, OUT:] = hess_ref[...]
    pl.semaphore_wait(barrier, n - 1)

    @pl.loop(1, n)
    def _(k):
        stats_copy(k).start()
        nodes_copy(k).start()
        bins_copy(k).start()

    left_acc[...] = jnp.zeros_like(left_acc)
    own_copy.wait()

    @pl.loop(0, n)
    def _(k):
        @pl.when(k > 0)
        def _():
            stats_copy(k).wait_recv()
            nodes_copy(k).wait_recv()
            bins_copy(k).wait_recv()

        stats = stats_all[k]
        label = jnp.broadcast_to(nodes_all[k], stats.shape)
        for node in range(NODES):
            weights[node * PAIR:(node + 1) * PAIR, :] = jnp.where(
                label == node, stats, 0.0).astype(jnp.bfloat16)

        @pl.loop(0, own)
        def _(feat):
            total = None
            for start in range(0, rows, ROW_TILE):
                size = min(ROW_TILE, rows - start)
                code = bins_all[k, pl.ds(feat, 1), start:start + size]
                high = (code >> 1).astype(jnp.float32).astype(jnp.bfloat16)
                low = (code & 1).astype(jnp.float32).astype(jnp.bfloat16)
                levels = lax.broadcasted_iota(jnp.int32, (HIGH, size), 0)
                levels = levels.astype(jnp.float32).astype(jnp.bfloat16)
                below = jnp.where(jnp.broadcast_to(high, (HIGH, size)) <= levels,
                                  jnp.ones((), jnp.bfloat16), jnp.zeros((), jnp.bfloat16))
                whole = weights[:, start:start + size]
                odd = whole * jnp.broadcast_to(low, (COLS, size))
                both = jnp.concatenate([whole - odd, odd], axis=0)
                part = lax.dot_general(both, below, OVER_LANES,
                                       preferred_element_type=jnp.float32)
                total = part if total is None else total + part
            left_acc[feat] = left_acc[feat] + total

    lane = lax.broadcasted_iota(jnp.int32, (COLS, HIGH), 1)
    width = gain_all.shape[-1]
    gain_lane = lax.broadcasted_iota(jnp.int32, (NODES, width), 1)

    def best_of(feat, gains):
        even, odd = left_acc[feat, :COLS], left_acc[feat, COLS:]
        left_odd = even + odd
        left_even = even + jnp.where(lane == 0, 0.0, pltpu.roll(odd, 1, axis=1))
        whole = jnp.broadcast_to(left_odd[:, HIGH - 1:], (COLS, HIGH))
        base = score(whole)
        gain = jnp.maximum(score(left_even) + score(whole - left_even) - base,
                           score(left_odd) + score(whole - left_odd) - base)
        best = jnp.max(gain, axis=1, keepdims=True)
        return jnp.where(gain_lane == me * own + feat,
                         jnp.broadcast_to(best, (NODES, width)), gains)

    gain_all[0] = lax.fori_loop(0, own, best_of, jnp.zeros((NODES, width), jnp.float32))

    @pl.loop(1, n)
    def _(k):
        gain_copy(k).start()

    @pl.loop(1, n)
    def _(k):
        gain_copy(k).wait_recv()

    out_ref[...] = jnp.sum(gain_all[...], axis=0)[:, :out_ref.shape[1]]

    @pl.loop(1, n)
    def _(k):
        stats_copy(k).wait_send()
        nodes_copy(k).wait_send()
        bins_copy(k).wait_send()
        gain_copy(k).wait_send()


def shards(bins, grads, hess, nodes, row_count):
    n = lax.axis_size("dp")
    feats, rows = bins.shape
    own = feats // n
    assert n & (n - 1) == 0 and own * n == feats
    width = -(-feats // LANES) * LANES
    vmem = pl.BlockSpec(memory_space=pltpu.VMEM)
    dma = pltpu.SemaphoreType.DMA
    return pl.pallas_call(
        functools.partial(kernel, n),
        out_shape=jax.ShapeDtypeStruct((NODES, feats), jnp.float32),
        in_specs=[pl.BlockSpec(memory_space=pl.ANY), vmem, vmem, vmem,
                  pl.BlockSpec(memory_space=pltpu.SMEM)],
        out_specs=vmem,
        scratch_shapes=[
            pltpu.VMEM((n, own, rows), jnp.int32),
            pltpu.VMEM((n, PAIR, rows), jnp.float32),
            pltpu.VMEM((n, 1, rows), jnp.int32),
            pltpu.VMEM((COLS, rows), jnp.bfloat16),
            pltpu.VMEM((own, 2 * COLS, HIGH), jnp.float32),
            pltpu.VMEM((n, NODES, width), jnp.float32),
            dma,
        ] + [dma((n,))] * 8,
        compiler_params=pltpu.CompilerParams(
            collective_id=0, has_side_effects=True, vmem_limit_bytes=40 << 20),
        name="histogram_gain",
    )(bins.reshape(n, own, rows), grads, hess, nodes.reshape(1, rows), row_count)


def solution(mesh):
    in_specs = (P("feat", "dp"), P(None, "dp"), P(None, "dp"), P("dp"), P("dp"))
    out_specs = P(None, "feat")
    return jax.shard_map(shards, mesh=mesh, in_specs=in_specs, out_specs=out_specs, check_vma=False)
```

time: 325 us -> 94.5 us (0.29)
  matrix products: 126 us -> 0 us
  waiting for transfers between devices: 92.5 us -> 0 us
  Pallas kernels: 0 us -> 89.1 us
  local copies, waits for them, and re-layouts: 61.4 us -> 4.47 us
  other arithmetic: 15.4 us -> 0 us
  between operations: 13.4 us -> 0.67 us
  blocking collectives: 12.7 us -> 0 us
    dot_general x24 -> x0, matrix products: 126 us -> none  [one_group(): jnp.einsum('cr,fbr->cfb', weighted, onehot, preferred_element_type=jnp.fl...]
    unnamed x2 -> x0, waiting for transfers between devices: 92.5 us -> none
    pallas_call x0 -> x1, Pallas kernels: none -> 89.1 us  [shards(): pl.pallas_call(functools.partial(kernel, n), out_shape=jax.ShapeDtypeStru...]
    dynamic_slice x30 -> x0, local copies, waits for them, and re-layouts: 22.4 us -> none  [the longest x24 20.3 us: one_group(): lax.dynamic_slice(bins, (feat_first, row_start), (feat_group, row_block))]
    all_gather x1 -> x0, blocking collectives: 12.7 us -> none  [shards(): best_gain = lax.all_gather(own_best, 'dp', axis=1, tiled=True)]
    another operation x5 -> x0, other arithmetic: 11.7 us -> none
    unnamed x3 -> x9, local copies, waits for them, and re-layouts: 15.6 us -> 4.47 us
    while x1 -> x0, local copies, waits for them, and re-layouts: 8.86 us -> none  [shards(): lax.fori_loop(0, n_blocks, one_block, jnp.zeros((col_width, feat_count, B...]
  transfers between devices with their start and end apart: 1 -> 0, of which waited for: 1 -> 0; matrix products, arithmetic and copies ran while one was open for 0% -> 0% of each run, Pallas kernels for 0% -> 0%
where the time goes in v1:
time: 94.5 us; the launch traced here: 94.2 us
  Pallas kernels  89.1 us (94%)
  local copies, waits for them, and re-layouts  4.47 us (5%)
    pallas_call x1, Pallas kernels, shards(): pl.pallas_call(functools.partial(kernel, n), out_shape=jax.ShapeDtypeStru...  89.1 us
    unnamed x9, local copies, waits for them, and re-layouts  4.47 us

profile of v1, /device:TPU:0, one launch (start us, length us, event | category | flops | bytes accessed | tf_op | source)
XLA Modules:
  0.0 94.2 jit_solution(6176031038923961229)
XLA Ops:
  0.7 0.0 copy-start
  0.7 1.4 %copy-done = s32[128,3072]{1,0:T(8,128)S(1)} copy-done((s32[128,3072]{1,0:T(8,128)S(1)}, s32[128,3072]{1,0:T(8,128)}, u32[]{:S(2)}) %copy-start) | copy-done | bytes 1572888
  2.1 0.0 copy-start.1
  2.1 0.9 copy-done.1
  3.0 0.0 copy-start.2
  3.0 0.9 copy-done.2
  3.8 0.0 copy-start.3
  3.8 0.7 copy-done.3
  4.6 89.1 %histogram_gain.1 = f32[4,128]{1,0:T(4,128)S(1)} custom-call(s32[8,16,3072]{2,1,0:T(8,128)S(1)} %bitcast.2, f32[8,3072]{1,0:T(8,128)S(1)} %copy-done.1, f32[8,3072]{1,0:T(8,128)S(1)} %copy-done.2, s32[1,3072]{1,0:T(1,128)S(1)} %bitcast.3, s32[1]{0:T(128)S(6)} %copy.7.count_ref), custom_call_target="tpu_custom_call" | custom-call | tf_op jit(solution)/shard_map/histogram_gain/pallas_call | solution.py:161
  93.6 0.6 copy.8
Async XLA Ops:
  0.7 1.4 %copy-start = (s32[128,3072]{1,0:T(8,128)S(1)}, s32[128,3072]{1,0:T(8,128)}, u32[]{:S(2)}) copy-start(s32[128,3072]{1,0:T(8,128)} %param.5) | copy-start | bytes 4718596
  2.1 0.9 copy-start.1
  3.0 0.9 copy-start.2
  3.8 0.7 copy-start.3

commit v2 on v1

--- a/solution.py
+++ b/solution.py
@@ -1,4 +1,5 @@
 import functools
+import math
 
 import jax
 import jax.numpy as jnp
@@ -25,56 +26,96 @@
     return jnp.sum(grad_sum * grad_sum / (hess_sum + 1.0), axis=1)
 
 
+def flip(index, k, size):
+    other, bit = 0, 1
+    while bit < size:
+        other = other + ((index // bit + k // bit) % 2) * bit
+        bit *= 2
+    return other
+
+
 def kernel(n, bins_ref, grads_ref, hess_ref, nodes_ref, count_ref, out_ref,
-           bins_all, stats_all, nodes_all, weights, left_acc, gain_all,
-           own_sem, bins_send, bins_recv, stats_send, stats_recv,
-           nodes_send, nodes_recv, gain_send, gain_recv):
+           bins_all, stats_all, weights, left_acc, gain_all,
+           own_sem, bins_send, bins_recv, direct_send, pass_send, stats_recv,
+           gain_send, gain_recv):
     own, rows = bins_all.shape[1:]
+    parts = stats_all.shape[1]
+    span = rows // parts
     me = lax.axis_index("dp")
+    group = lax.axis_index("feat")
+    my_part = group % parts
 
     def partner(k):
-        other, bit = 0, 1
-        while bit < n:
-            other = other + ((me // bit + k // bit) % 2) * bit
-            bit *= 2
-        return other
-
-    def remote(src, dst, send, recv, k):
+        return flip(me, k, n)
+
+    def sibling(j):
+        return group - my_part + flip(my_part, j, parts)
+
+    def remote(src, dst, send, recv, dp, feat):
         return pltpu.make_async_remote_copy(
-            src_ref=src, dst_ref=dst, send_sem=send.at[k], recv_sem=recv.at[k],
-            device_id={"dp": partner(k)}, device_id_type=pl.DeviceIdType.MESH)
+            src_ref=src, dst_ref=dst, send_sem=send, recv_sem=recv,
+            device_id={"dp": dp, "feat": feat}, device_id_type=pl.DeviceIdType.MESH)
 
     def bins_copy(k):
-        return remote(bins_ref.at[partner(k)], bins_all.at[k], bins_send, bins_recv, k)
-
-    def stats_copy(k):
-        return remote(stats_all.at[0], stats_all.at[k], stats_send, stats_recv, k)
-
-    def nodes_copy(k):
-        return remote(nodes_all.at[0], nodes_all.at[k], nodes_send, nodes_recv, k)
+        return remote(bins_ref.at[partner(k)], bins_all.at[k],
+                      bins_send.at[k], bins_recv.at[k], partner(k), group)
 
     def gain_copy(k):
-        return remote(gain_all.at[0], gain_all.at[k], gain_send, gain_recv, k)
+        return remote(gain_all.at[0], gain_all.at[k],
+                      gain_send.at[k], gain_recv.at[k], partner(k), group)
+
+    def pair_copy():
+        return remote(stats_all.at[0], stats_all.at[1],
+                      direct_send.at[1], stats_recv.at[1, 0], partner(1), group)
+
+    def part_copy(k):
+        return remote(stats_all.at[0, my_part], stats_all.at[k, my_part],
+                      direct_send.at[k], stats_recv.at[k, 0], partner(k), group)
+
+    def pass_copy(k, side, j):
+        return remote(stats_all.at[k, my_part], stats_all.at[k + side, my_part],
+                      pass_send.at[k, side, j], stats_recv.at[k + side, j],
+                      partner(side), sibling(j))
 
     own_copy = pltpu.make_async_copy(bins_ref.at[me], bins_all.at[0], own_sem)
     own_copy.start()
     barrier = pltpu.get_barrier_semaphore()
 
-    @pl.loop(1, n)
-    def _(k):
-        pl.semaphore_signal(barrier, inc=1, device_id={"dp": partner(k)},
+    def greet(dp, feat):
+        pl.semaphore_signal(barrier, inc=1, device_id={"dp": dp, "feat": feat},
                             device_id_type=pl.DeviceIdType.MESH)
 
-    slot_index = lax.broadcasted_iota(jnp.int32, (1, rows), 1)
-    nodes_all[0] = jnp.where(slot_index < count_ref[0], nodes_ref[...], NODES)
-    stats_all[0, :OUT] = grads_ref[...]
-    stats_all[0, OUT:] = hess_ref[...]
-    pl.semaphore_wait(barrier, n - 1)
-
-    @pl.loop(1, n)
-    def _(k):
-        stats_copy(k).start()
-        nodes_copy(k).start()
+    @pl.loop(1, n)
+    def _(k):
+        greet(partner(k), group)
+
+    @pl.loop(1, parts)
+    def _(j):
+        greet(me, sibling(j))
+        greet(partner(1), sibling(j))
+
+    for part in range(parts):
+        first = part * span
+        stats_all[0, part, :OUT, :span] = grads_ref[:, first:first + span]
+        stats_all[0, part, OUT:, :span] = hess_ref[:, first:first + span]
+        for row in range(span // LANES):
+            at = first + row * LANES
+            slot_index = at + lax.broadcasted_iota(jnp.int32, (1, LANES), 1)
+            stats_all[0, part, row:row + 1, span:] = jnp.where(
+                slot_index < count_ref[0], nodes_ref[:, at:at + LANES],
+                NODES).astype(jnp.float32)
+        stats_all[0, part, span // LANES:, span:] = jnp.zeros(
+            (PAIR - span // LANES, LANES), jnp.float32)
+    pl.semaphore_wait(barrier, n - 1 + 2 * (parts - 1))
+
+    pair_copy().start()
+
+    @pl.loop(1, n // 2)
+    def _(half):
+        part_copy(2 * half).start()
+
+    @pl.loop(1, n)
+    def _(k):
         bins_copy(k).start()
 
     left_acc[...] = jnp.zeros_like(left_acc)
@@ -84,15 +125,42 @@
     def _(k):
         @pl.when(k > 0)
         def _():
-            stats_copy(k).wait_recv()
-            nodes_copy(k).wait_recv()
             bins_copy(k).wait_recv()
 
-        stats = stats_all[k]
-        label = jnp.broadcast_to(nodes_all[k], stats.shape)
-        for node in range(NODES):
-            weights[node * PAIR:(node + 1) * PAIR, :] = jnp.where(
-                label == node, stats, 0.0).astype(jnp.bfloat16)
+        @pl.when(k == 1)
+        def _():
+            pair_copy().wait_recv()
+
+            @pl.loop(1, n // 2)
+            def _(half):
+                part_copy(2 * half).wait_recv()
+                pass_copy(2 * half, 1, 0).start()
+
+                @pl.loop(1, parts)
+                def _(j):
+                    pass_copy(2 * half, 0, j).start()
+                    pass_copy(2 * half, 1, j).start()
+
+        @pl.when(k > 1)
+        def _():
+            @pl.when(k % 2 == 1)
+            def _():
+                pass_copy(k - 1, 1, 0).wait_recv()
+
+            @pl.loop(1, parts)
+            def _(j):
+                pass_copy(k - k % 2, k % 2, j).wait_recv()
+
+        for part in range(parts):
+            for row in range(span // LANES):
+                block = slice(row * LANES, (row + 1) * LANES)
+                stats = stats_all[k, part, :, block]
+                label = jnp.broadcast_to(
+                    stats_all[k, part, row:row + 1, span:], (PAIR, LANES))
+                at = part * span + row * LANES
+                for node in range(NODES):
+                    weights[node * PAIR:(node + 1) * PAIR, at:at + LANES] = jnp.where(
+                        label == node, stats, 0.0).astype(jnp.bfloat16)
 
         @pl.loop(0, own)
         def _(feat):
@@ -142,10 +210,20 @@
 
     out_ref[...] = jnp.sum(gain_all[...], axis=0)[:, :out_ref.shape[1]]
 
-    @pl.loop(1, n)
-    def _(k):
-        stats_copy(k).wait_send()
-        nodes_copy(k).wait_send()
+    pair_copy().wait_send()
+
+    @pl.loop(1, n // 2)
+    def _(half):
+        part_copy(2 * half).wait_send()
+        pass_copy(2 * half, 1, 0).wait_send()
+
+        @pl.loop(1, parts)
+        def _(j):
+            pass_copy(2 * half, 0, j).wait_send()
+            pass_copy(2 * half, 1, j).wait_send()
+
+    @pl.loop(1, n)
+    def _(k):
         bins_copy(k).wait_send()
         gain_copy(k).wait_send()
 
@@ -155,6 +233,8 @@
     feats, rows = bins.shape
     own = feats // n
     assert n & (n - 1) == 0 and own * n == feats
+    parts = math.gcd(lax.axis_size("feat"), rows // LANES)
+    assert n > 1 and parts & (parts - 1) == 0 and rows % (parts * LANES) == 0
     width = -(-feats // LANES) * LANES
     vmem = pl.BlockSpec(memory_space=pltpu.VMEM)
     dma = pltpu.SemaphoreType.DMA
@@ -166,13 +246,13 @@
         out_specs=vmem,
         scratch_shapes=[
             pltpu.VMEM((n, own, rows), jnp.int32),
-            pltpu.VMEM((n, PAIR, rows), jnp.float32),
-            pltpu.VMEM((n, 1, rows), jnp.int32),
+            pltpu.VMEM((n, parts, PAIR, rows // parts + LANES), jnp.float32),
             pltpu.VMEM((COLS, rows), jnp.bfloat16),
             pltpu.VMEM((own, 2 * COLS, HIGH), jnp.float32),
             pltpu.VMEM((n, NODES, width), jnp.float32),
-            dma,
-        ] + [dma((n,))] * 8,
+            dma, dma((n,)), dma((n,)), dma((n,)), dma((n, 2, parts)), dma((n, parts)),
+            dma((n,)), dma((n,)),
+        ],
         compiler_params=pltpu.CompilerParams(
             collective_id=0, has_side_effects=True, vmem_limit_bytes=40 << 20),
         name="histogram_gain",

time: 94.5 us -> 75.1 us (0.79)
  Pallas kernels: 89.1 us -> 69.7 us
    pallas_call x1, Pallas kernels: 89.1 us -> 69.7 us  [shards(): pl.pallas_call(functools.partial(kernel, n), out_shape=jax.ShapeDtypeStru...]
where the time goes in v2:
time: 75.1 us; the launch traced here: 74.8 us
  Pallas kernels  69.7 us (93%)
  local copies, waits for them, and re-layouts  4.47 us (6%)
    pallas_call x1, Pallas kernels, shards(): pl.pallas_call(functools.partial(kernel, n), out_shape=jax.ShapeDtypeStru...  69.7 us
    unnamed x9, local copies, waits for them, and re-layouts  4.47 us

profile of v2, /device:TPU:0, one launch (start us, length us, event | category | flops | bytes accessed | tf_op | source)
XLA Modules:
  0.0 74.8 jit_solution(1596386783845297246)
XLA Ops:
  0.7 0.0 copy-start
  0.7 1.4 %copy-done = s32[128,3072]{1,0:T(8,128)S(1)} copy-done((s32[128,3072]{1,0:T(8,128)S(1)}, s32[128,3072]{1,0:T(8,128)}, u32[]{:S(2)}) %copy-start) | copy-done | bytes 1572888
  2.1 0.0 copy-start.1
  2.1 0.9 %copy-done.1 = f32[8,3072]{1,0:T(8,128)S(1)} copy-done((f32[8,3072]{1,0:T(8,128)S(1)}, f32[8,3072]{1,0:T(8,128)}, u32[]{:S(2)}) %copy-start.1) | copy-done | bytes 98328
  3.0 0.0 copy-start.2
  3.0 0.9 %copy-done.2 = f32[8,3072]{1,0:T(8,128)S(1)} copy-done((f32[8,3072]{1,0:T(8,128)S(1)}, f32[8,3072]{1,0:T(8,128)}, u32[]{:S(2)}) %copy-start.2) | copy-done | bytes 98328
  3.8 0.0 copy-start.3
  3.8 0.7 copy-done.3
  4.6 69.7 %histogram_gain.1 = f32[4,128]{1,0:T(4,128)S(1)} custom-call(s32[8,16,3072]{2,1,0:T(8,128)S(1)} %bitcast.2, f32[8,3072]{1,0:T(8,128)S(1)} %copy-done.1, f32[8,3072]{1,0:T(8,128)S(1)} %copy-done.2, s32[1,3072]{1,0:T(1,128)S(1)} %bitcast.3, s32[1]{0:T(128)S(6)} %copy.7.count_ref), custom_call_target="tpu_custom_call" | custom-call | tf_op jit(solution)/shard_map/histogram_gain/pallas_call | solution.py:241
  74.3 0.6 copy.8
Async XLA Ops:
  0.7 1.4 %copy-start = (s32[128,3072]{1,0:T(8,128)S(1)}, s32[128,3072]{1,0:T(8,128)}, u32[]{:S(2)}) copy-start(s32[128,3072]{1,0:T(8,128)} %param.5) | copy-start | bytes 4718596
  2.1 0.9 %copy-start.1 = (f32[8,3072]{1,0:T(8,128)S(1)}, f32[8,3072]{1,0:T(8,128)}, u32[]{:S(2)}) copy-start(f32[8,3072]{1,0:T(8,128)} %grads_ref.1) | copy-start | bytes 294916
  3.0 0.9 %copy-start.2 = (f32[8,3072]{1,0:T(8,128)S(1)}, f32[8,3072]{1,0:T(8,128)}, u32[]{:S(2)}) copy-start(f32[8,3072]{1,0:T(8,128)} %hess_ref.1) | copy-start | bytes 294916
  3.8 0.7 copy-start.3

commit v3 on v2

--- a/solution.py
+++ b/solution.py
@@ -162,7 +162,7 @@
                     weights[node * PAIR:(node + 1) * PAIR, at:at + LANES] = jnp.where(
                         label == node, stats, 0.0).astype(jnp.bfloat16)
 
-        @pl.loop(0, own)
+        @pl.loop(0, own, unroll=min(own, 8))
         def _(feat):
             total = None
             for start in range(0, rows, ROW_TILE):
@@ -198,7 +198,7 @@
         return jnp.where(gain_lane == me * own + feat,
                          jnp.broadcast_to(best, (NODES, width)), gains)
 
-    gain_all[0] = lax.fori_loop(0, own, best_of, jnp.zeros((NODES, width), jnp.float32))
+    gain_all[0] = lax.fori_loop(0, own, best_of, jnp.zeros((NODES, width), jnp.float32), unroll=min(own, 4))
 
     @pl.loop(1, n)
     def _(k):

time: 75.1 us -> 60.5 us (0.81)
  Pallas kernels: 69.7 us -> 55.1 us
    pallas_call x1, Pallas kernels: 69.7 us -> 55.1 us  [shards(): pl.pallas_call(functools.partial(kernel, n), out_shape=jax.ShapeDtypeStru...]
where the time goes in v3:
time: 60.5 us; the launch traced here: 60.2 us
  Pallas kernels  55.1 us (91%)
  local copies, waits for them, and re-layouts  4.47 us (7%)
  between operations  0.67 us (1%)
    pallas_call x1, Pallas kernels, shards(): pl.pallas_call(functools.partial(kernel, n), out_shape=jax.ShapeDtypeStru...  55.1 us
    unnamed x9, local copies, waits for them, and re-layouts  4.47 us

profile of v3, /device:TPU:0, one launch (start us, length us, event | category | flops | bytes accessed | tf_op | source)
XLA Modules:
  0.0 60.2 jit_solution(3233544407968296253)
XLA Ops:
  0.7 0.0 copy-start
  0.7 1.4 %copy-done = s32[128,3072]{1,0:T(8,128)S(1)} copy-done((s32[128,3072]{1,0:T(8,128)S(1)}, s32[128,3072]{1,0:T(8,128)}, u32[]{:S(2)}) %copy-start) | copy-done | bytes 1572888
  2.1 0.0 copy-start.1
  2.1 0.9 %copy-done.1 = f32[8,3072]{1,0:T(8,128)S(1)} copy-done((f32[8,3072]{1,0:T(8,128)S(1)}, f32[8,3072]{1,0:T(8,128)}, u32[]{:S(2)}) %copy-start.1) | copy-done | bytes 98328
  3.0 0.0 copy-start.2
  3.0 0.9 %copy-done.2 = f32[8,3072]{1,0:T(8,128)S(1)} copy-done((f32[8,3072]{1,0:T(8,128)S(1)}, f32[8,3072]{1,0:T(8,128)}, u32[]{:S(2)}) %copy-start.2) | copy-done | bytes 98328
  3.8 0.0 copy-start.3
  3.8 0.7 %copy-done.3 = s32[3072]{0:T(1024)S(1)} copy-done((s32[3072]{0:T(1024)S(1)}, s32[3072]{0:T(1024)}, u32[]{:S(2)}) %copy-start.3) | copy-done | bytes 12312
  4.6 55.1 %histogram_gain.1 = f32[4,128]{1,0:T(4,128)S(1)} custom-call(s32[8,16,3072]{2,1,0:T(8,128)S(1)} %bitcast.2, f32[8,3072]{1,0:T(8,128)S(1)} %copy-done.1, f32[8,3072]{1,0:T(8,128)S(1)} %copy-done.2, s32[1,3072]{1,0:T(1,128)S(1)} %bitcast.3, s32[1]{0:T(128)S(6)} %copy.7.count_ref), custom_call_target="tpu_custom_call" | custom-call | tf_op jit(solution)/shard_map/histogram_gain/pallas_call | solution.py:241
  59.6 0.6 copy.8
Async XLA Ops:
  0.7 1.4 %copy-start = (s32[128,3072]{1,0:T(8,128)S(1)}, s32[128,3072]{1,0:T(8,128)}, u32[]{:S(2)}) copy-start(s32[128,3072]{1,0:T(8,128)} %param.5) | copy-start | bytes 4718596
  2.1 0.9 %copy-start.1 = (f32[8,3072]{1,0:T(8,128)S(1)}, f32[8,3072]{1,0:T(8,128)}, u32[]{:S(2)}) copy-start(f32[8,3072]{1,0:T(8,128)} %grads_ref.1) | copy-start | bytes 294916
  3.0 0.9 %copy-start.2 = (f32[8,3072]{1,0:T(8,128)S(1)}, f32[8,3072]{1,0:T(8,128)}, u32[]{:S(2)}) copy-start(f32[8,3072]{1,0:T(8,128)} %hess_ref.1) | copy-start | bytes 294916
  3.8 0.7 %copy-start.3 = (s32[3072]{0:T(1024)S(1)}, s32[3072]{0:T(1024)}, u32[]{:S(2)}) copy-start(s32[3072]{0:T(1024)} %param.8) | copy-start | bytes 36868

commit v4 on v3

--- a/solution.py
+++ b/solution.py
@@ -40,6 +40,7 @@
            gain_send, gain_recv):
     own, rows = bins_all.shape[1:]
     parts = stats_all.shape[1]
+    halves = bins_send.shape[1]
     span = rows // parts
     me = lax.axis_index("dp")
     group = lax.axis_index("feat")
@@ -56,9 +57,10 @@
             src_ref=src, dst_ref=dst, send_sem=send, recv_sem=recv,
             device_id={"dp": dp, "feat": feat}, device_id_type=pl.DeviceIdType.MESH)
 
-    def bins_copy(k):
-        return remote(bins_ref.at[partner(k)], bins_all.at[k],
-                      bins_send.at[k], bins_recv.at[k], partner(k), group)
+    def bins_copy(k, half):
+        some = pl.ds(half * (own // halves), own // halves)
+        return remote(bins_ref.at[partner(k), some], bins_all.at[k, some],
+                      bins_send.at[k, half], bins_recv.at[k, half], partner(k), group)
 
     def gain_copy(k):
         return remote(gain_all.at[0], gain_all.at[k],
@@ -116,17 +118,14 @@
 
     @pl.loop(1, n)
     def _(k):
-        bins_copy(k).start()
+        for half in range(halves):
+            bins_copy(k, half).start()
 
     left_acc[...] = jnp.zeros_like(left_acc)
     own_copy.wait()
 
     @pl.loop(0, n)
     def _(k):
-        @pl.when(k > 0)
-        def _():
-            bins_copy(k).wait_recv()
-
         @pl.when(k == 1)
         def _():
             pair_copy().wait_recv()
@@ -162,25 +161,32 @@
                     weights[node * PAIR:(node + 1) * PAIR, at:at + LANES] = jnp.where(
                         label == node, stats, 0.0).astype(jnp.bfloat16)
 
-        @pl.loop(0, own, unroll=min(own, 8))
-        def _(feat):
-            total = None
-            for start in range(0, rows, ROW_TILE):
-                size = min(ROW_TILE, rows - start)
-                code = bins_all[k, pl.ds(feat, 1), start:start + size]
-                high = (code >> 1).astype(jnp.float32).astype(jnp.bfloat16)
-                low = (code & 1).astype(jnp.float32).astype(jnp.bfloat16)
-                levels = lax.broadcasted_iota(jnp.int32, (HIGH, size), 0)
-                levels = levels.astype(jnp.float32).astype(jnp.bfloat16)
-                below = jnp.where(jnp.broadcast_to(high, (HIGH, size)) <= levels,
-                                  jnp.ones((), jnp.bfloat16), jnp.zeros((), jnp.bfloat16))
-                whole = weights[:, start:start + size]
-                odd = whole * jnp.broadcast_to(low, (COLS, size))
-                both = jnp.concatenate([whole - odd, odd], axis=0)
-                part = lax.dot_general(both, below, OVER_LANES,
-                                       preferred_element_type=jnp.float32)
-                total = part if total is None else total + part
-            left_acc[feat] = left_acc[feat] + total
+        @pl.loop(0, halves)
+        def _(half):
+            @pl.when(k > 0)
+            def _():
+                bins_copy(k, half).wait_recv()
+
+            @pl.loop(0, own // halves, unroll=min(own // halves, 8))
+            def _(at):
+                feat = half * (own // halves) + at
+                total = None
+                for start in range(0, rows, ROW_TILE):
+                    size = min(ROW_TILE, rows - start)
+                    code = bins_all[k, pl.ds(feat, 1), start:start + size]
+                    high = (code >> 1).astype(jnp.float32).astype(jnp.bfloat16)
+                    low = (code & 1).astype(jnp.float32).astype(jnp.bfloat16)
+                    levels = lax.broadcasted_iota(jnp.int32, (HIGH, size), 0)
+                    levels = levels.astype(jnp.float32).astype(jnp.bfloat16)
+                    below = jnp.where(jnp.broadcast_to(high, (HIGH, size)) <= levels,
+                                      jnp.ones((), jnp.bfloat16), jnp.zeros((), jnp.bfloat16))
+                    whole = weights[:, start:start + size]
+                    odd = whole * jnp.broadcast_to(low, (COLS, size))
+                    both = jnp.concatenate([whole - odd, odd], axis=0)
+                    part = lax.dot_general(both, below, OVER_LANES,
+                                           preferred_element_type=jnp.float32)
+                    total = part if total is None else total + part
+                left_acc[feat] = left_acc[feat] + total
 
     lane = lax.broadcasted_iota(jnp.int32, (COLS, HIGH), 1)
     width = gain_all.shape[-1]
@@ -224,7 +230,8 @@
 
     @pl.loop(1, n)
     def _(k):
-        bins_copy(k).wait_send()
+        for half in range(halves):
+            bins_copy(k, half).wait_send()
         gain_copy(k).wait_send()
 
 
@@ -235,6 +242,7 @@
     assert n & (n - 1) == 0 and own * n == feats
     parts = math.gcd(lax.axis_size("feat"), rows // LANES)
     assert n > 1 and parts & (parts - 1) == 0 and rows % (parts * LANES) == 0
+    halves = 2 if own % 16 == 0 else 1
     width = -(-feats // LANES) * LANES
     vmem = pl.BlockSpec(memory_space=pltpu.VMEM)
     dma = pltpu.SemaphoreType.DMA
@@ -250,7 +258,7 @@
             pltpu.VMEM((COLS, rows), jnp.bfloat16),
             pltpu.VMEM((own, 2 * COLS, HIGH), jnp.float32),
             pltpu.VMEM((n, NODES, width), jnp.float32),
-            dma, dma((n,)), dma((n,)), dma((n,)), dma((n, 2, parts)), dma((n, parts)),
+            dma, dma((n, halves)), dma((n, halves)), dma((n,)), dma((n, 2, parts)), dma((n, parts)),
             dma((n,)), dma((n,)),
         ],
         compiler_params=pltpu.CompilerParams(

time: 60.5 us -> 58.7 us (0.970)
  Pallas kernels: 55.1 us -> 53.3 us
    pallas_call x1, Pallas kernels: 55.1 us -> 53.3 us  [shards(): pl.pallas_call(functools.partial(kernel, n), out_shape=jax.ShapeDtypeStru...]
where the time goes in v4:
time: 58.7 us; the launch traced here: 58.5 us
  Pallas kernels  53.3 us (91%)
  local copies, waits for them, and re-layouts  4.47 us (8%)
  between operations  0.67 us (1%)
    pallas_call x1, Pallas kernels, shards(): pl.pallas_call(functools.partial(kernel, n), out_shape=jax.ShapeDtypeStru...  53.3 us
    unnamed x9, local copies, waits for them, and re-layouts  4.47 us

profile of v4, /device:TPU:0, one launch (start us, length us, event | category | flops | bytes accessed | tf_op | source)
XLA Modules:
  0.0 58.5 jit_solution(5981565618821552890)
XLA Ops:
  0.7 0.0 copy-start
  0.7 1.4 %copy-done = s32[128,3072]{1,0:T(8,128)S(1)} copy-done((s32[128,3072]{1,0:T(8,128)S(1)}, s32[128,3072]{1,0:T(8,128)}, u32[]{:S(2)}) %copy-start) | copy-done | bytes 1572888
  2.1 0.0 copy-start.1
  2.1 0.9 %copy-done.1 = f32[8,3072]{1,0:T(8,128)S(1)} copy-done((f32[8,3072]{1,0:T(8,128)S(1)}, f32[8,3072]{1,0:T(8,128)}, u32[]{:S(2)}) %copy-start.1) | copy-done | bytes 98328
  3.0 0.0 copy-start.2
  3.0 0.9 %copy-done.2 = f32[8,3072]{1,0:T(8,128)S(1)} copy-done((f32[8,3072]{1,0:T(8,128)S(1)}, f32[8,3072]{1,0:T(8,128)}, u32[]{:S(2)}) %copy-start.2) | copy-done | bytes 98328
  3.8 0.0 copy-start.3
  3.8 0.7 %copy-done.3 = s32[3072]{0:T(1024)S(1)} copy-done((s32[3072]{0:T(1024)S(1)}, s32[3072]{0:T(1024)}, u32[]{:S(2)}) %copy-start.3) | copy-done | bytes 12312
  4.6 53.3 %histogram_gain.1 = f32[4,128]{1,0:T(4,128)S(1)} custom-call(s32[8,16,3072]{2,1,0:T(8,128)S(1)} %bitcast.2, f32[8,3072]{1,0:T(8,128)S(1)} %copy-done.1, f32[8,3072]{1,0:T(8,128)S(1)} %copy-done.2, s32[1,3072]{1,0:T(1,128)S(1)} %bitcast.3, s32[1]{0:T(128)S(6)} %copy.7.count_ref), custom_call_target="tpu_custom_call" | custom-call | tf_op jit(solution)/shard_map/histogram_gain/pallas_call | solution.py:249
  57.9 0.6 copy.8
Async XLA Ops:
  0.7 1.4 %copy-start = (s32[128,3072]{1,0:T(8,128)S(1)}, s32[128,3072]{1,0:T(8,128)}, u32[]{:S(2)}) copy-start(s32[128,3072]{1,0:T(8,128)} %param.5) | copy-start | bytes 4718596
  2.1 0.9 %copy-start.1 = (f32[8,3072]{1,0:T(8,128)S(1)}, f32[8,3072]{1,0:T(8,128)}, u32[]{:S(2)}) copy-start(f32[8,3072]{1,0:T(8,128)} %grads_ref.1) | copy-start | bytes 294916
  3.0 0.9 %copy-start.2 = (f32[8,3072]{1,0:T(8,128)S(1)}, f32[8,3072]{1,0:T(8,128)}, u32[]{:S(2)}) copy-start(f32[8,3072]{1,0:T(8,128)} %hess_ref.1) | copy-start | bytes 294916
  3.8 0.7 %copy-start.3 = (s32[3072]{0:T(1024)S(1)}, s32[3072]{0:T(1024)}, u32[]{:S(2)}) copy-start(s32[3072]{0:T(1024)} %param.8) | copy-start | bytes 36868
